TPU v7x, 256 devices: a whole 4x4x8 slice. The times are simulated.
256 devices in a mesh: dp: 32 (over y, x, core), shard: 8 (over z).
Axes of the slice: x: 4, y: 4, z: 8, core: 2. Of those that a mesh axis runs over, the one named last changes fastest.
Arguments:
- grads: bfloat16 [2, 32, 4096, 4096], P(None, 'dp', 'shard'), may hold values from -0.5 to 0.5
- basis: float32 [2, 4096, 256], P(None, 'shard'), may hold values from -0.375 to 0.375
- weight: float32 [2, 8, 32, 16, 4096], P(None, 'shard', 'dp'), may hold values from -6 to 6
- moment_m: float32 [2, 4096, 256], P(None, 'dp'), may hold values from -6 to 6
- moment_v: float32 [2, 4096, 256], P(None, 'dp'), may hold values from 0.25 to 4
Outputs:
- new_weight: float32 [2, 8, 32, 16, 4096], P(None, 'shard', 'dp')
- new_m: float32 [2, 4096, 256], P(None, 'dp')
- new_v: float32 [2, 4096, 256], P(None, 'dp')
- new_basis: float32 [2, 4096, 256], P(None, 'shard')
All inputs are finite; a program needn't handle non-finite values.
Results may differ from a plain program's by a relative error of at most 0.0036.
Values may be sent and summed in bfloat16 or wider, within the bound.
A program may use at most 64 MiB of HBM per device.

v0:
```python
import jax
import jax.numpy as jnp
from jax import lax
from jax.sharding import PartitionSpec as P

MATS = 2
NS_STEPS = 5


def adam_step(moment_m, moment_v, projected):
    next_m = 0.9 * moment_m + 0.1 * projected
    next_v = 0.999 * moment_v + 0.001 * projected * projected
    update = 2.0 * (next_m / (1.0 - 0.9**10)) / (jnp.sqrt(next_v / (1.0 - 0.999**10)) + 1e-08)
    return (next_m, next_v, update)


def ns_turn(iterate, gram):
    return 1.5 * iterate - 0.5 * jnp.dot(iterate, gram, precision=lax.Precision.HIGHEST)


def shards(grads, basis, weight, moment_m, moment_v):
    group_index = lax.axis_index("dp")
    rows_weight = weight.shape[3]
    weights_out, firsts, seconds, bases = ([], [], [], [])
    for matrix in range(MATS):
        gradient = grads[matrix, 0]
        basis_local = basis[matrix]
        basis_bf = basis_local.astype(jnp.bfloat16)
        partial_sum = lax.psum_scatter(
            lax.dot_general(
                gradient, basis_bf, (((0,), (0,)), ((), ())), preferred_element_type=jnp.float32
            ),
            "dp",
            scatter_dimension=0,
            tiled=True,
        )
        projected = lax.psum(partial_sum, "shard")
        next_m, next_v, update = adam_step(moment_m[matrix], moment_v[matrix], projected)
        full_update = lax.all_gather(update, "dp", axis=0, tiled=True)
        basis_rows = lax.dynamic_slice_in_dim(
            basis_local, group_index * rows_weight, rows_weight, 0
        )
        delta = jnp.dot(basis_rows, full_update.T, precision=lax.Precision.HIGHEST)
        weights_out.append((weight[matrix, 0, 0] - delta).reshape(weight.shape[1:]))
        projected_bf = projected.astype(jnp.bfloat16)
        refresh_part = jnp.dot(
            gradient,
            lax.all_gather(projected_bf, "dp", axis=0, tiled=True),
            preferred_element_type=jnp.float32,
        )
        refresh = lax.psum(refresh_part, "dp")
        total_sq = lax.psum(jnp.sum(refresh * refresh), "shard")
        iterate = refresh / jnp.sqrt(total_sq + 1e-06)
        first_turn = 0
        for step in range(first_turn, NS_STEPS):
            gram = lax.psum(
                jnp.dot(iterate.T, iterate, precision=lax.Precision.HIGHEST).astype(jnp.bfloat16),
                "shard",
            ).astype(jnp.float32)
            iterate = ns_turn(iterate, gram)
        bases.append(iterate)
        firsts.append(next_m)
        seconds.append(next_v)
    return (jnp.stack(weights_out), jnp.stack(firsts), jnp.stack(seconds), jnp.stack(bases))


def solution(mesh):
    placed = (
        P(None, "dp", "shard", None),
        P(None, "shard", None),
        P(None, "shard", "dp", None, None),
        P(None, "dp", None),
        P(None, "dp", None),
    )
    return jax.shard_map(
        shards,
        mesh=mesh,
        in_specs=placed,
        out_specs=(
            P(None, "shard", "dp", None, None),
            P(None, "dp", None),
            P(None, "dp", None),
            P(None, "shard", None),
        ),
        check_vma=False,
    )
```

profile of v0, /device:TPU:1, one launch (start us, length us, event | category | flops | bytes accessed | tf_op | source)
XLA Modules:
  0.0 1018.5 jit_solution(8599303258596466312)
XLA Ops:
  7.2 5.5 fusion.4
  14.0 5.5 fusion.8
  19.6 85.4 %reduce-scatter.5.cloned.1.call-done = f32[128,256]{1,0:T(8,128)} async-done(((f32[4096,256]{1,0:T(8,128)}), f32[128,256]{1,0:T(8,128)}) %reduce-scatter.5.cloned.1.call-update) | async-done | bytes 131088 | tf_op jit(solution)/shard_map/reduce_scatter | solution.py:29
  104.9 93.3 %reduce-scatter.3.cloned.1.call-done = f32[128,256]{1,0:T(8,128)} async-done(((f32[4096,256]{1,0:T(8,128)}), f32[128,256]{1,0:T(8,128)}) %reduce-scatter.3.cloned.1.call-update) | async-done | bytes 131088 | tf_op jit(solution)/shard_map/reduce_scatter | solution.py:29
  198.3 71.4 %all-reduce.18.cloned.1.call-done = (f32[128,256]{1,0:T(8,128)}, f32[128,256]{1,0:T(8,128)}) async-done(((f32[128,256]{1,0:T(8,128)}, f32[128,256]{1,0:T(8,128)}), (f32[128,256]{1,0:T(8,128)}, f32[128,256]{1,0:T(8,128)})) %all-reduce.18.cloned.1.call-update) | async-done | bytes 262160 | tf_op jit(solution)/shard_map/psum | solution.py:37
  269.8 2.0 add_divide_fusion.1
  272.4 52.9 %all-gather.9.cloned.1.call-done = bf16[4096,256]{1,0:T(8,128)(2,1)} async-done(((bf16[128,256]{1,0:T(8,128)(2,1)}), bf16[4096,256]{1,0:T(8,128)(2,1)}) %all-gather.9.cloned.1.call-update) | async-done | bytes 2097168 | tf_op jit(solution)/shard_map/all_gather | solution.py:48
  325.3 4.9 fusion.14
  330.2 46.1 %all-gather.11.cloned.1.call-done = bf16[4096,256]{1,0:T(8,128)(2,1)} async-done(((bf16[128,256]{1,0:T(8,128)(2,1)}), bf16[4096,256]{1,0:T(8,128)(2,1)}) %all-gather.11.cloned.1.call-update) | async-done | bytes 2097168 | tf_op jit(solution)/shard_map/all_gather | solution.py:48
  376.3 4.9 fusion.17
  381.3 114.6 %all-reduce.16.cloned.1.call-done = (f32[512,256]{0,1:T(8,128)}, f32[512,256]{0,1:T(8,128)}) async-done(((f32[512,256]{0,1:T(8,128)}, f32[512,256]{0,1:T(8,128)}), (f32[512,256]{0,1:T(8,128)}, f32[512,256]{0,1:T(8,128)})) %all-reduce.16.cloned.1.call-update) | async-done | bytes 1048592 | tf_op jit(solution)/shard_map/psum | solution.py:51
  495.8 2.0 multiply_reduce_fusion
  497.8 14.3 %all-reduce.1 = (f32[]{:T(128)}, f32[]{:T(128)}) all-reduce(f32[]{:T(128)} %get-tuple-element.36, f32[]{:T(128)} %get-tuple-element.37), channel_id=1, replica_groups=mesh['dp'=32,'shard'=8] {'shard'}, use_global_device_ids=true, to_apply=%region_14.0 | all-reduce | flops 2 | bytes 16 | tf_op jit(solution)/shard_map/psum | solution.py:52
  513.5 2.5 convolution_convert_fusion.4
  516.1 2.5 convolution_convert_fusion.9
  518.6 68.6 %all-reduce.28.cloned.1.call-done = (bf16[256,256]{1,0:T(8,128)(2,1)}, bf16[256,256]{1,0:T(8,128)(2,1)}) async-done(((bf16[256,256]{1,0:T(8,128)(2,1)}, bf16[256,256]{1,0:T(8,128)(2,1)}), (bf16[256,256]{1,0:T(8,128)(2,1)}, bf16[256,256]{1,0:T(8,128)(2,1)})) %all-reduce.28.cloned.1.call-update) | async-done | bytes 262160 | tf_op jit(solution)/shard_map/psum | solution.py:56
  587.2 1.4 fusion.31
  588.6 1.4 fusion.25
  592.8 71.3 %all-reduce.26.cloned.1.call-done = (bf16[256,256]{1,0:T(8,128)(2,1)}, bf16[256,256]{1,0:T(8,128)(2,1)}) async-done(((bf16[256,256]{1,0:T(8,128)(2,1)}, bf16[256,256]{1,0:T(8,128)(2,1)}), (bf16[256,256]{1,0:T(8,128)(2,1)}, bf16[256,256]{1,0:T(8,128)(2,1)})) %all-reduce.26.cloned.1.call-update) | async-done | bytes 262160 | tf_op jit(solution)/shard_map/psum | solution.py:56
  664.2 1.4 fusion.24
  665.6 1.4 fusion.30
  669.6 71.5 %all-reduce.24.cloned.1.call-done = (bf16[256,256]{1,0:T(8,128)(2,1)}, bf16[256,256]{1,0:T(8,128)(2,1)}) async-done(((bf16[256,256]{1,0:T(8,128)(2,1)}, bf16[256,256]{1,0:T(8,128)(2,1)}), (bf16[256,256]{1,0:T(8,128)(2,1)}, bf16[256,256]{1,0:T(8,128)(2,1)})) %all-reduce.24.cloned.1.call-update) | async-done | bytes 262160 | tf_op jit(solution)/shard_map/psum | solution.py:56
  742.5 1.4 fusion.29
  746.5 71.5 %all-reduce.22.cloned.1.call-done = (bf16[256,256]{1,0:T(8,128)(2,1)}, bf16[256,256]{1,0:T(8,128)(2,1)}) async-done(((bf16[256,256]{1,0:T(8,128)(2,1)}, bf16[256,256]{1,0:T(8,128)(2,1)}), (bf16[256,256]{1,0:T(8,128)(2,1)}, bf16[256,256]{1,0:T(8,128)(2,1)})) %all-reduce.22.cloned.1.call-update) | async-done | bytes 262160 | tf_op jit(solution)/shard_map/psum | solution.py:56
  818.0 1.4 fusion.22
  819.4 1.4 fusion.28
  826.8 68.2 %all-reduce.20.cloned.1.call-done = (bf16[256,256]{1,0:T(8,128)(2,1)}, bf16[256,256]{1,0:T(8,128)(2,1)}) async-done(((bf16[256,256]{1,0:T(8,128)(2,1)}, bf16[256,256]{1,0:T(8,128)(2,1)}), (bf16[256,256]{1,0:T(8,128)(2,1)}, bf16[256,256]{1,0:T(8,128)(2,1)})) %all-reduce.20.cloned.1.call-update) | async-done | bytes 262160 | tf_op jit(solution)/shard_map/psum | solution.py:56
  896.4 1.4 fusion.27
  899.2 53.3 %all-gather.5.cloned.1.call-done = f32[4096,256]{1,0:T(8,128)} async-done(((f32[128,256]{1,0:T(8,128)}), f32[4096,256]{1,0:T(8,128)}) %all-gather.5.cloned.1.call-update) | async-done | bytes 4194320 | tf_op jit(solution)/shard_map/all_gather | solution.py:39
  952.4 5.7 fusion.1
  958.1 47.4 %all-gather.7.cloned.1.call-done = f32[4096,256]{1,0:T(8,128)} async-done(((f32[128,256]{1,0:T(8,128)}), f32[4096,256]{1,0:T(8,128)}) %all-gather.7.cloned.1.call-update) | async-done | bytes 4194320 | tf_op jit(solution)/shard_map/all_gather | solution.py:39
  1005.5 5.7 fusion
  (53 shorter events, 21.1 us)
Async XLA Ops:
  7.2 97.8 %reduce-scatter.5.cloned.1.call-start = ((), (), s32[]{:S(2)}) async-start(), calls=%async_computation.4 | async-start | bytes 4325376 | tf_op jit(solution)/shard_map/reduce_scatter | solution.py:29
  12.8 1.2 copy-start
  12.8 185.5 %reduce-scatter.3.cloned.1.call-start = ((), (), s32[]{:S(2)}) async-start(), calls=%async_computation.2 | async-start | bytes 4325376 | tf_op jit(solution)/shard_map/reduce_scatter | solution.py:29
  19.5 250.3 %copy-start.4 = (f32[2,128,256]{2,1,0:T(8,128)S(1)}, f32[2,128,256]{2,1,0:T(8,128)}, u32[]{:S(2)}) copy-start(f32[2,128,256]{2,1,0:T(8,128)} %param.8) | copy-start | bytes 786436
  19.5 250.3 %copy-start.5 = (f32[2,128,256]{2,1,0:T(8,128)S(1)}, f32[2,128,256]{2,1,0:T(8,128)}, u32[]{:S(2)}) copy-start(f32[2,128,256]{2,1,0:T(8,128)} %param.9) | copy-start | bytes 786436
  19.5 250.2 %all-reduce.18.cloned.1.call-start = ((), (), s32[]{:S(2)}) async-start(), calls=%async_computation.9 | async-start | bytes 524288 | tf_op jit(solution)/shard_map/psum | solution.py:37
  198.3 127.0 %all-gather.9.cloned.1.call-start = ((), (), s32[]{:S(2)}) async-start(), calls=%async_computation.6 | async-start | bytes 2162688 | tf_op jit(solution)/shard_map/all_gather | solution.py:48
  271.7 104.5 %all-gather.11.cloned.1.call-start = ((), (), s32[]{:S(2)}) async-start(), calls=%async_computation.7 | async-start | bytes 2162688 | tf_op jit(solution)/shard_map/all_gather | solution.py:48
  272.3 223.5 %all-reduce.16.cloned.1.call-start = ((), (), s32[]{:S(2)}) async-start(), calls=%async_computation.8 | async-start | bytes 2097152 | tf_op jit(solution)/shard_map/psum | solution.py:51
  381.2 206.0 %all-reduce.28.cloned.1.call-start = ((), (), s32[]{:S(2)}) async-start(), calls=%async_computation.14 | async-start | bytes 524288 | tf_op jit(solution)/shard_map/psum | solution.py:56
  495.8 91.4 %copy-start.3 = (f32[512,256]{0,1:T(8,128)S(1)}, f32[512,256]{0,1:T(8,128)}, u32[]{:S(2)}) copy-start(f32[512,256]{0,1:T(8,128)} %get-tuple-element.9) | copy-start | bytes 1572868
  497.8 90.8 %copy-start.2 = (f32[512,256]{0,1:T(8,128)S(1)}, f32[512,256]{0,1:T(8,128)}, u32[]{:S(2)}) copy-start(f32[512,256]{0,1:T(8,128)} %get-tuple-element.8) | copy-start | bytes 1572868
  518.6 145.6 %all-reduce.26.cloned.1.call-start = ((), (), s32[]{:S(2)}) async-start(), calls=%async_computation.13 | async-start | bytes 524288 | tf_op jit(solution)/shard_map/psum | solution.py:56
  592.6 148.5 %all-reduce.24.cloned.1.call-start = ((), (), s32[]{:S(2)}) async-start(), calls=%async_computation.12 | async-start | bytes 524288 | tf_op jit(solution)/shard_map/psum | solution.py:56
  669.5 148.5 %all-reduce.22.cloned.1.call-start = ((), (), s32[]{:S(2)}) async-start(), calls=%async_computation.11 | async-start | bytes 524288 | tf_op jit(solution)/shard_map/psum | solution.py:56
  746.4 148.5 %all-reduce.20.cloned.1.call-start = ((), (), s32[]{:S(2)}) async-start(), calls=%async_computation.10 | async-start | bytes 524288 | tf_op jit(solution)/shard_map/psum | solution.py:56
  823.3 129.1 %all-gather.5.cloned.1.call-start = ((), (), s32[]{:S(2)}) async-start(), calls=%async_computation.3 | async-start | bytes 4325376 | tf_op jit(solution)/shard_map/all_gather | solution.py:39
  823.9 181.6 %all-gather.7.cloned.1.call-start = ((), (), s32[]{:S(2)}) async-start(), calls=%async_computation.5 | async-start | bytes 4325376 | tf_op jit(solution)/shard_map/all_gather | solution.py:39
  825.9 126.5 %copy-start.1 = (f32[2,1,1,16,4096]{4,3,2,1,0:T(8,128)S(1)}, f32[2,1,1,16,4096]{4,3,2,1,0:T(8,128)}, u32[]{:S(2)}) copy-start(f32[2,1,1,16,4096]{4,3,2,1,0:T(8,128)} %param.7) | copy-start | bytes 1572868
Sparse Core Ops, SparseCore 0:
  12.9 91.9 reduce-scatter.4
  108.9 89.3 reduce-scatter.2
  200.6 69.0 all-reduce.17
  272.7 52.5 all-gather.8
  328.3 47.9 all-gather.10
  381.3 114.4 all-reduce.15
  518.7 68.4 all-reduce.27
  592.7 71.3 all-reduce.25
  669.6 71.3 all-reduce.23
  746.5 71.3 all-reduce.21
  823.5 71.4 all-reduce.19
  897.4 54.9 all-gather.4
  955.0 50.4 all-gather.6
where the time goes:
time: 1020 us
  waiting for transfers between devices  917 us (90%)
  matrix products  61.3 us (6%)
  between operations  15.4 us (2%)
  blocking collectives  14.3 us (1%)
    psum x5, waiting for transfers between devices, shards(): lax.psum(jnp.dot(iterate.T, iterate, precision=lax.Precision.HIGHEST).ast...  351 us
    reduce_scatter x2, waiting for transfers between devices, shards(): lax.psum_scatter(lax.dot_general(gradient, basis_bf, (((0,), (0,)), ((),...  179 us
    psum x1, waiting for transfers between devices, shards(): refresh = lax.psum(refresh_part, 'dp')  115 us
    all_gather x2, waiting for transfers between devices, shards(): full_update = lax.all_gather(update, 'dp', axis=0, tiled=True)  101 us
    all_gather x2, waiting for transfers between devices, shards(): lax.all_gather(projected_bf, 'dp', axis=0, tiled=True)  99 us
    psum x1, waiting for transfers between devices, shards(): projected = lax.psum(partial_sum, 'shard')  71.4 us
  transfers between devices with their start and end apart: 13, of which 13 were waited for; matrix products, arithmetic and copies ran while one was open for 2% of the time, Pallas kernels for 0%

commit v1 on v0

--- a/solution.py
+++ b/solution.py
@@ -34,7 +34,11 @@
             scatter_dimension=0,
             tiled=True,
         )
-        projected = lax.psum(partial_sum, "shard")
+        projected = partial_sum
+        for hop in (1, 2, 4):
+            projected = projected + lax.ppermute(
+                projected, "shard", [(dev, dev ^ hop) for dev in range(8)]
+            )
         next_m, next_v, update = adam_step(moment_m[matrix], moment_v[matrix], projected)
         full_update = lax.all_gather(update, "dp", axis=0, tiled=True)
         basis_rows = lax.dynamic_slice_in_dim(

time: 1020 us -> 946 us (0.927)
  waiting for transfers between devices: 917 us -> 823 us
  starting transfers between devices: 0.93 us -> 19.3 us
    psum x1 -> x0, waiting for transfers between devices: 71.4 us -> none  [shards(): projected = lax.psum(partial_sum, 'shard')]
    reduce_scatter x2, waiting for transfers between devices: 179 us -> 159 us  [shards(): lax.psum_scatter(lax.dot_general(gradient, basis_bf, (((0,), (0,)), ((),...]
    all_gather x2, waiting for transfers between devices: 99 us -> 79.5 us  [shards(): lax.all_gather(projected_bf, 'dp', axis=0, tiled=True)]
    ppermute x0 -> x6, starting transfers between devices: none -> 18.4 us  [shards(): lax.ppermute(projected, 'shard', [(dev, dev ^ hop) for dev in range(8)])]
    ppermute x0 -> x6, waiting for transfers between devices: none -> 18.1 us  [shards(): lax.ppermute(projected, 'shard', [(dev, dev ^ hop) for dev in range(8)])]
  transfers between devices with their start and end apart: 13 -> 18, of which waited for: 13 -> 18; matrix products, arithmetic and copies ran while one was open for 2% -> 3% of each run, Pallas kernels for 0% -> 0%
where the time goes in v1:
time: 946 us; the launch traced here: 945 us
  waiting for transfers between devices  823 us (87%)
  matrix products  60.4 us (6%)
  starting transfers between devices  19.3 us (2%)
  between operations  15.8 us (2%)
  blocking collectives  14.3 us (2%)
  other arithmetic  10 us (1%)
    psum x5, waiting for transfers between devices, shards(): lax.psum(jnp.dot(iterate.T, iterate, precision=lax.Precision.HIGHEST).ast...  350 us
    reduce_scatter x2, waiting for transfers between devices, shards(): lax.psum_scatter(lax.dot_general(gradient, basis_bf, (((0,), (0,)), ((),...  159 us
    psum x1, waiting for transfers between devices, shards(): refresh = lax.psum(refresh_part, 'dp')  115 us
    all_gather x2, waiting for transfers between devices, shards(): full_update = lax.all_gather(update, 'dp', axis=0, tiled=True)  101 us
    all_gather x2, waiting for transfers between devices, shards(): lax.all_gather(projected_bf, 'dp', axis=0, tiled=True)  79.5 us
  transfers between devices with their start and end apart: 18, of which 18 were waited for; matrix products, arithmetic and copies ran while one was open for 3% of the time, Pallas kernels for 0%

profile of v1, /device:TPU:1, one launch (start us, length us, event | category | flops | bytes accessed | tf_op | source)
XLA Modules:
  0.0 945.1 jit_solution(8075530683474858713)
XLA Ops:
  7.2 5.6 fusion.4
  14.1 5.4 fusion.8
  19.6 85.4 %reduce-scatter.5.cloned.1.call-done = f32[128,256]{1,0:T(8,128)} async-done(((f32[4096,256]{1,0:T(8,128)}), f32[128,256]{1,0:T(8,128)}) %reduce-scatter.5.cloned.1.call-update) | async-done | bytes 131088 | tf_op jit(solution)/shard_map/reduce_scatter | solution.py:29
  106.3 2.7 collective-permute-done.3
  110.0 2.4 collective-permute-start.4
  112.3 3.9 collective-permute-done.4
  116.2 5.5 collective-permute-start.5
  121.7 2.5 collective-permute-done.5
  124.9 73.4 %reduce-scatter.3.cloned.1.call-done = f32[128,256]{1,0:T(8,128)} async-done(((f32[4096,256]{1,0:T(8,128)}), f32[128,256]{1,0:T(8,128)}) %reduce-scatter.3.cloned.1.call-update) | async-done | bytes 131088 | tf_op jit(solution)/shard_map/reduce_scatter | solution.py:29
  199.6 2.7 collective-permute-done
  203.3 2.4 collective-permute-start.1
  205.7 3.9 collective-permute-done.1
  209.5 5.5 collective-permute-start.2
  215.1 2.5 collective-permute-done.2
  218.3 33.4 %all-gather.11.cloned.1.call-done = bf16[4096,256]{1,0:T(8,128)(2,1)} async-done(((bf16[128,256]{1,0:T(8,128)(2,1)}), bf16[4096,256]{1,0:T(8,128)(2,1)}) %all-gather.11.cloned.1.call-update) | async-done | bytes 2097168 | tf_op jit(solution)/shard_map/all_gather | solution.py:52
  251.6 4.9 fusion.17
  256.6 46.1 %all-gather.9.cloned.1.call-done = bf16[4096,256]{1,0:T(8,128)(2,1)} async-done(((bf16[128,256]{1,0:T(8,128)(2,1)}), bf16[4096,256]{1,0:T(8,128)(2,1)}) %all-gather.9.cloned.1.call-update) | async-done | bytes 2097168 | tf_op jit(solution)/shard_map/all_gather | solution.py:52
  302.6 4.9 fusion.14
  307.6 114.6 %all-reduce.14.cloned.1.call-done = (f32[512,256]{0,1:T(8,128)}, f32[512,256]{0,1:T(8,128)}) async-done(((f32[512,256]{0,1:T(8,128)}, f32[512,256]{0,1:T(8,128)}), (f32[512,256]{0,1:T(8,128)}, f32[512,256]{0,1:T(8,128)})) %all-reduce.14.cloned.1.call-update) | async-done | bytes 1048592 | tf_op jit(solution)/shard_map/psum | solution.py:55
  424.2 14.3 %all-reduce.1 = (f32[]{:T(128)}, f32[]{:T(128)}) all-reduce(f32[]{:T(128)} %get-tuple-element.36, f32[]{:T(128)} %get-tuple-element.37), channel_id=1, replica_groups=mesh['dp'=32,'shard'=8] {'shard'}, use_global_device_ids=true, to_apply=%region_12.0 | all-reduce | flops 2 | bytes 16 | tf_op jit(solution)/shard_map/psum | solution.py:56
  439.2 2.5 convolution_convert_fusion.4
  442.5 2.5 convolution_convert_fusion.9
  445.2 68.4 %all-reduce.24.cloned.1.call-done = (bf16[256,256]{1,0:T(8,128)(2,1)}, bf16[256,256]{1,0:T(8,128)(2,1)}) async-done(((bf16[256,256]{1,0:T(8,128)(2,1)}, bf16[256,256]{1,0:T(8,128)(2,1)}), (bf16[256,256]{1,0:T(8,128)(2,1)}, bf16[256,256]{1,0:T(8,128)(2,1)})) %all-reduce.24.cloned.1.call-update) | async-done | bytes 262160 | tf_op jit(solution)/shard_map/psum | solution.py:60
  518.2 71.5 %all-reduce.22.cloned.1.call-done = (bf16[256,256]{1,0:T(8,128)(2,1)}, bf16[256,256]{1,0:T(8,128)(2,1)}) async-done(((bf16[256,256]{1,0:T(8,128)(2,1)}, bf16[256,256]{1,0:T(8,128)(2,1)}), (bf16[256,256]{1,0:T(8,128)(2,1)}, bf16[256,256]{1,0:T(8,128)(2,1)})) %all-reduce.22.cloned.1.call-update) | async-done | bytes 262160 | tf_op jit(solution)/shard_map/psum | solution.py:60
  595.1 71.6 %all-reduce.20.cloned.1.call-done = (bf16[256,256]{1,0:T(8,128)(2,1)}, bf16[256,256]{1,0:T(8,128)(2,1)}) async-done(((bf16[256,256]{1,0:T(8,128)(2,1)}, bf16[256,256]{1,0:T(8,128)(2,1)}), (bf16[256,256]{1,0:T(8,128)(2,1)}, bf16[256,256]{1,0:T(8,128)(2,1)})) %all-reduce.20.cloned.1.call-update) | async-done | bytes 262160 | tf_op jit(solution)/shard_map/psum | solution.py:60
  672.1 71.6 %all-reduce.18.cloned.1.call-done = (bf16[256,256]{1,0:T(8,128)(2,1)}, bf16[256,256]{1,0:T(8,128)(2,1)}) async-done(((bf16[256,256]{1,0:T(8,128)(2,1)}, bf16[256,256]{1,0:T(8,128)(2,1)}), (bf16[256,256]{1,0:T(8,128)(2,1)}, bf16[256,256]{1,0:T(8,128)(2,1)})) %all-reduce.18.cloned.1.call-update) | async-done | bytes 262160 | tf_op jit(solution)/shard_map/psum | solution.py:60
  749.1 2.0 add_divide_fusion.1
  753.7 67.0 %all-reduce.16.cloned.1.call-done = (bf16[256,256]{1,0:T(8,128)(2,1)}, bf16[256,256]{1,0:T(8,128)(2,1)}) async-done(((bf16[256,256]{1,0:T(8,128)(2,1)}, bf16[256,256]{1,0:T(8,128)(2,1)}), (bf16[256,256]{1,0:T(8,128)(2,1)}, bf16[256,256]{1,0:T(8,128)(2,1)})) %all-reduce.16.cloned.1.call-update) | async-done | bytes 262160 | tf_op jit(solution)/shard_map/psum | solution.py:60
  824.8 53.4 %all-gather.7.cloned.1.call-done = f32[4096,256]{1,0:T(8,128)} async-done(((f32[128,256]{1,0:T(8,128)}), f32[4096,256]{1,0:T(8,128)}) %all-gather.7.cloned.1.call-update) | async-done | bytes 4194320 | tf_op jit(solution)/shard_map/all_gather | solution.py:43
  878.2 5.7 fusion
  883.9 47.8 %all-gather.5.cloned.1.call-done = f32[4096,256]{1,0:T(8,128)} async-done(((f32[128,256]{1,0:T(8,128)}), f32[4096,256]{1,0:T(8,128)}) %all-gather.5.cloned.1.call-update) | async-done | bytes 4194320 | tf_op jit(solution)/shard_map/all_gather | solution.py:43
  931.7 5.7 fusion.1
  (66 shorter events, 37.7 us)
Async XLA Ops:
  7.2 97.8 %reduce-scatter.5.cloned.1.call-start = ((), (), s32[]{:S(2)}) async-start(), calls=%async_computation.4 | async-start | bytes 4325376 | tf_op jit(solution)/shard_map/reduce_scatter | solution.py:29
  12.8 1.2 copy-start
  12.9 185.5 %reduce-scatter.3.cloned.1.call-start = ((), (), s32[]{:S(2)}) async-start(), calls=%async_computation.2 | async-start | bytes 4325376 | tf_op jit(solution)/shard_map/reduce_scatter | solution.py:29
  19.5 232.1 %all-gather.11.cloned.1.call-start = ((), (), s32[]{:S(2)}) async-start(), calls=%async_computation.7 | async-start | bytes 2162688 | tf_op jit(solution)/shard_map/all_gather | solution.py:52
  105.0 4.0 collective-permute-start.3
  110.0 6.2 collective-permute-start.4
  116.2 8.0 collective-permute-start.5
  124.9 177.8 %all-gather.9.cloned.1.call-start = ((), (), s32[]{:S(2)}) async-start(), calls=%async_computation.6 | async-start | bytes 2162688 | tf_op jit(solution)/shard_map/all_gather | solution.py:52
  198.3 4.0 collective-permute-start
  203.3 6.2 collective-permute-start.1
  209.5 8.0 collective-permute-start.2
  218.2 204.0 %all-reduce.14.cloned.1.call-start = ((), (), s32[]{:S(2)}) async-start(), calls=%async_computation.8 | async-start | bytes 2097152 | tf_op jit(solution)/shard_map/psum | solution.py:55
  307.6 206.0 %all-reduce.24.cloned.1.call-start = ((), (), s32[]{:S(2)}) async-start(), calls=%async_computation.13 | async-start | bytes 524288 | tf_op jit(solution)/shard_map/psum | solution.py:60
  422.2 91.4 %copy-start.3 = (f32[512,256]{0,1:T(8,128)S(1)}, f32[512,256]{0,1:T(8,128)}, u32[]{:S(2)}) copy-start(f32[512,256]{0,1:T(8,128)} %get-tuple-element.8) | copy-start | bytes 1572868
  441.7 74.6 %copy-start.2 = (f32[512,256]{0,1:T(8,128)S(1)}, f32[512,256]{0,1:T(8,128)}, u32[]{:S(2)}) copy-start(f32[512,256]{0,1:T(8,128)} %get-tuple-element.9) | copy-start | bytes 1572868
  445.0 144.7 %all-reduce.22.cloned.1.call-start = ((), (), s32[]{:S(2)}) async-start(), calls=%async_computation.12 | async-start | bytes 524288 | tf_op jit(solution)/shard_map/psum | solution.py:60
  513.6 2.7 copy-start.4
  518.1 148.5 %all-reduce.20.cloned.1.call-start = ((), (), s32[]{:S(2)}) async-start(), calls=%async_computation.11 | async-start | bytes 524288 | tf_op jit(solution)/shard_map/psum | solution.py:60
  595.1 148.6 %all-reduce.18.cloned.1.call-start = ((), (), s32[]{:S(2)}) async-start(), calls=%async_computation.10 | async-start | bytes 524288 | tf_op jit(solution)/shard_map/psum | solution.py:60
  672.0 148.6 %all-reduce.16.cloned.1.call-start = ((), (), s32[]{:S(2)}) async-start(), calls=%async_computation.9 | async-start | bytes 524288 | tf_op jit(solution)/shard_map/psum | solution.py:60
  749.0 129.2 %all-gather.7.cloned.1.call-start = ((), (), s32[]{:S(2)}) async-start(), calls=%async_computation.5 | async-start | bytes 4325376 | tf_op jit(solution)/shard_map/all_gather | solution.py:43
  751.1 180.6 %all-gather.5.cloned.1.call-start = ((), (), s32[]{:S(2)}) async-start(), calls=%async_computation.3 | async-start | bytes 4325376 | tf_op jit(solution)/shard_map/all_gather | solution.py:43
  751.8 126.5 %copy-start.1 = (f32[2,1,1,16,4096]{4,3,2,1,0:T(8,128)S(1)}, f32[2,1,1,16,4096]{4,3,2,1,0:T(8,128)}, u32[]{:S(2)}) copy-start(f32[2,1,1,16,4096]{4,3,2,1,0:T(8,128)} %param.7) | copy-start | bytes 1572868
Sparse Core Ops, SparseCore 0:
  13.0 91.9 reduce-scatter.4
  108.9 89.3 reduce-scatter.2
  201.5 50.1 all-gather.10
  254.6 47.9 all-gather.8
  307.7 114.4 all-reduce.13
  445.1 68.4 all-reduce.23
  518.3 71.3 all-reduce.21
  595.2 71.4 all-reduce.19
  672.2 71.4 all-reduce.17
  749.1 71.4 all-reduce.15
  823.2 54.9 all-gather.6
  881.2 50.4 all-gather.4
